TPU v7x, 256 devices: a whole 4x4x8 slice. The times are simulated.
256 devices in a mesh: rows: 64 (over x_hi, y, z), grp: 4 (over x_lo, core).
Axes of the slice: x: 4 (x_hi: 2, x_lo: 2; x = x_hi * 2 + x_lo), y: 4, z: 8, core: 2. Of those that a mesh axis runs over, the one named last changes fastest.
Arguments:
- table: float32 [524288, 256], P(('rows', 'grp')), may hold values from -1.5 to 1.5
- hot_slot: int32 [4096], P(('rows', 'grp')), may hold values from 0 to 2047, as said below
- cold_row: int32 [256, 256, 8], P(('rows', 'grp')), may hold values from 0 to 2047, as said below
- cold_bag: int32 [256, 256, 8], P(('rows', 'grp')), may hold values from 0 to 511
- hot_pick: int32 [65536, 8], P(('rows', 'grp')), may hold values from 0 to 4095
- dense: float32 [65536, 256], P(('rows', 'grp')), may hold values from -6 to 6
- label: int32 [65536], P(('rows', 'grp')), may hold values 0 or 1
Outputs:
- pooled: float32 [65536, 256], P(('rows', 'grp'))
- new_table: float32 [524288, 256], P(('rows', 'grp'))
- hot_new: float32 [4096, 256], replicated
Inputs may be any that keep to these rules, and one draw needn't show every extreme that they name: `hot_slot`: distinct within each device's block of 16 entries; hot row h lies in the shard of device h // 16. `cold_row`: a cold slot never names a hot row of its owner. `cold_bag`: a value of 256 or more marks an empty slot.
All inputs are finite; a program needn't handle non-finite values. No bound on the sum of `label` on one device may be relied on, other than what follows from the above.
Results may differ from a plain program's by a relative error of at most 0.0029.
Values may be sent and summed in bfloat16 or wider, within the bound.
A program may use at most 64 MiB of HBM per device.

v0:
```python
import jax
import jax.numpy as jnp
from jax import lax
from jax.sharding import PartitionSpec as P


def split_up(value, dim, peers):
    shape = value.shape
    blocks = value.reshape(*shape[:dim], peers, shape[dim] // peers, *shape[dim + 1 :])
    return jnp.moveaxis(blocks, dim, 0)


def laid_out(blocks, dim):
    blocks = jnp.moveaxis(blocks, 0, dim)
    shape = blocks.shape
    return blocks.reshape(*shape[:dim], shape[dim] * shape[dim + 1], *shape[dim + 2 :])


def exchange_both(value, axis, axes, splits, concats):
    sizes = [lax.axis_size(a) for a in axes]
    blocks = split_up(value, splits[0], sizes[0])
    blocks = jnp.moveaxis(split_up(blocks, splits[1] + 1, sizes[1]), 0, 1)
    inside = blocks.shape[2:]
    blocks = blocks.reshape(-1, *inside)
    blocks = lax.all_to_all(blocks, axis, split_axis=0, concat_axis=0, tiled=True)
    blocks = laid_out(blocks.reshape(*sizes, *inside), concats[0] + 1)
    return laid_out(blocks, concats[1])


def body(table, hot_slot, cold_row, cold_bag, hot_pick, dense, label):
    n_rows = lax.axis_size("rows")
    n_grp = lax.axis_size("grp")
    width = table.shape[1]
    samples = dense.shape[0]
    own_hot = hot_slot.shape[0]
    slots = cold_row.shape[1] * cold_row.shape[2]
    per_peer = cold_row.shape[2]
    rounded = table.astype(jnp.bfloat16)
    hot_full = lax.all_gather(table[hot_slot], ("rows", "grp"), axis=0, tiled=True)
    hot_copy = hot_full.astype(jnp.bfloat16)
    requests = cold_row[0].reshape(n_rows, n_grp, per_peer)
    arrived = exchange_both(requests, ("rows", "grp"), ("rows", "grp"), (0, 1), (0, 1))
    looked = rounded[arrived.reshape(-1)].reshape(n_rows, n_grp, per_peer, width)
    returned = lax.all_to_all(
        lax.all_to_all(looked, "rows", split_axis=0, concat_axis=0, tiled=True),
        "grp",
        split_axis=1,
        concat_axis=1,
        tiled=True,
    )
    flat_rows = returned.reshape(slots, width)
    bags = cold_bag[0].reshape(slots)
    selector = jnp.arange(samples, dtype=jnp.int32)[:, None] == bags[None, :]
    cold_pooled = jnp.dot(
        selector.astype(jnp.bfloat16), flat_rows, preferred_element_type=jnp.float32
    )
    hot_pooled = jnp.sum(hot_copy[hot_pick].astype(jnp.float32), axis=1)
    pooled = cold_pooled + hot_pooled
    score = jnp.sum(pooled * dense, axis=1) / width**0.5
    err = jax.nn.sigmoid(score) - label.astype(jnp.float32)
    grad = err[:, None] * dense
    slot_grad = lax.dot_general(
        selector.astype(jnp.float32),
        grad,
        (((0,), (0,)), ((), ())),
        precision=lax.Precision.HIGHEST,
        preferred_element_type=jnp.float32,
    )
    delivered = exchange_both(
        slot_grad.reshape(n_rows, n_grp, per_peer, width),
        ("rows", "grp"),
        ("rows", "grp"),
        (0, 1),
        (0, 1),
    )
    table_grad = jax.ops.segment_sum(
        delivered.reshape(slots, width), arrived.reshape(slots), num_segments=table.shape[0]
    )
    hot_total = hot_copy.shape[0]
    spread = jnp.repeat(grad, hot_pick.shape[1], axis=0)
    hot_local = jax.ops.segment_sum(spread, hot_pick.reshape(-1), num_segments=hot_total)
    summed = lax.psum(hot_local, ("rows", "grp"))
    start = lax.axis_index(("rows", "grp")) * own_hot
    own_grad = lax.dynamic_slice_in_dim(summed, start, own_hot, 0)
    table_grad = table_grad.at[hot_slot].add(own_grad)
    new_table = table - 0.1 * table_grad
    hot_new = hot_full - 0.1 * summed
    return (pooled, new_table, hot_new)


def solution(mesh):
    placed = (
        P(("rows", "grp"), None),
        P(("rows", "grp")),
        P(("rows", "grp"), None, None),
        P(("rows", "grp"), None, None),
        P(("rows", "grp"), None),
        P(("rows", "grp"), None),
        P(("rows", "grp")),
    )
    return jax.shard_map(
        body,
        mesh=mesh,
        in_specs=placed,
        out_specs=(P(("rows", "grp"), None), P(("rows", "grp"), None), P()),
        check_vma=False,
    )
```

profile of v0, /device:TPU:2, one launch (start us, length us, event | category | flops | bytes accessed | tf_op | source)
XLA Modules:
  0.0 783.1 jit_solution(3402326476514333365)
XLA Ops:
  7.2 0.0 all-gather.3.cloned.1.call-start
  7.2 0.7 compare_select_fusion.2
  7.9 0.0 copy-start.6
  7.9 0.5 copy-done.6
  8.4 2.8 gather_fusion.1
  11.2 0.0 all-gather.3.cloned.1.call-update
  11.2 1.5 copy.38
  12.7 14.7 %all-to-all-start = ((s32[256,1,1,8]{3,2,1,0:T(1,128)}), s32[256,1,1,8]{3,2,1,0:T(1,128)S(1)}, u32[]{:S(2)}, u32[]{:S(2)}) async-start(s32[256,1,1,8]{3,2,1,0:T(1,128)} %bitcast), calls=%async_computation | async-start | bytes 262144 | tf_op jit(solution)/shard_map/all_to_all | solution.py:25
  27.4 1.7 convert_element_type.14
  29.1 10.6 %all-to-all-done = s32[256,1,1,8]{3,2,1,0:T(1,128)S(1)} async-done(((s32[256,1,1,8]{3,2,1,0:T(1,128)}), s32[256,1,1,8]{3,2,1,0:T(1,128)S(1)}, u32[]{:S(2)}, u32[]{:S(2)}) %all-to-all-start) | async-done | bytes 8224 | tf_op jit(solution)/shard_map/all_to_all | solution.py:25
  39.6 0.2 reshape_reshape.6
  39.8 7.5 gather_fusion
  47.3 34.3 %all_to_all.20 = bf16[64,4,8,256]{3,2,1,0:T(8,128)(2,1)S(1)} all-to-all(bf16[64,4,8,256]{3,2,1,0:T(8,128)(2,1)S(1)} %bitcast.38), channel_id=1, replica_groups=mesh['rows'=64,'grp'=4] {'rows'}, dimensions={0} | all-to-all | bytes 2097152 | tf_op jit(solution)/shard_map/all_to_all | solution.py:45
  81.6 0.0 copy-start.1
  81.6 0.0 copy-start.2
  81.6 0.0 copy-start.4
  81.6 1.0 copy.39
  82.6 4.7 all-to-all-start.2
  87.3 0.0 copy-done.1
  87.3 0.8 copy.43
  88.2 0.0 copy-done.2
  88.2 0.1 copy.41
  88.3 0.1 reshape.82
  88.4 0.0 copy-done.4
  88.4 0.1 copy.37
  88.6 0.1 eq.16
  88.7 12.2 %all-to-all-done.2 = bf16[64,4,8,256]{3,2,0,1:T(8,128)(2,1)S(1)} async-done(((bf16[64,4,8,256]{3,2,0,1:T(8,128)(2,1)}), bf16[64,4,8,256]{3,2,0,1:T(8,128)(2,1)S(1)}, u32[]{:S(2)}, u32[]{:S(2)}) %all-to-all-start.2) | async-done | bytes 1048608 | tf_op jit(solution)/shard_map/all_to_all | solution.py:44
  100.9 1.1 copy.40
  102.0 330.1 %all-gather.3.cloned.1.call-done = f32[4096,256]{1,0:T(8,128)} async-done(((f32[16,256]{1,0:T(8,128)}), f32[4096,256]{1,0:T(8,128)}) %all-gather.3.cloned.1.call-update) | async-done | bytes 4194320 | tf_op jit(solution)/shard_map/all_gather | solution.py:39
  432.1 2.4 convert_element_type.15
  434.5 7.5 gather_fusion.2
  442.0 0.0 copy-start.5
  442.0 0.7 convert_reduce_fusion
  442.7 0.1 copy.42
  442.9 2.0 multiply_reduce_fusion
  444.9 0.0 copy-done.5
  444.9 0.1 broadcast_multiply_fusion
  445.0 3.2 fusion.7
  448.2 0.0 copy-start.3
  448.2 9.4 %all-to-all-start.3 = ((f32[256,1,1,8,256]{4,3,2,1,0:T(8,128)}), f32[256,1,1,8,256]{4,3,2,1,0:T(8,128)S(1)}, u32[]{:S(2)}, u32[]{:S(2)}) async-start(f32[256,1,1,8,256]{4,3,2,1,0:T(8,128)} %fusion.7), calls=%async_computation.3 | async-start | bytes 4194304 | tf_op jit(solution)/shard_map/all_to_all | solution.py:25
  457.5 0.2 all-reduce.2.cloned.1.call-start
  457.7 0.0 copy-done.3
  457.8 0.1 copy.45
  457.9 0.1 reshape.98
  458.0 13.8 %scatter_custom_fusion.1 = f32[4096,256]{1,0:T(8,128)} fusion(s32[2048]{0:T(1024)S(1)} %reshape.98, f32[]{:T(128)} %constant.15.clone.1, f32[256,256]{1,0:T(8,128)S(1)} %broadcast_multiply_fusion), kind=kCustom, calls=%fused_computation.10 | custom fusion | flops 524288 | bytes 4456452 | tf_op jit(solution)/shard_map/scatter-add | solution.py:81
  471.8 0.0 all-reduce.2.cloned.1.call-update
  471.9 0.2 reshape.90
  472.0 0.8 copy.46
  472.9 277.2 %all-reduce.2.cloned.1.call-done = f32[4096,256]{1,0:T(8,128)} async-done(((f32[4096,256]{1,0:T(8,128)}), f32[4096,256]{1,0:T(8,128)}) %all-reduce.2.cloned.1.call-update) | async-done | bytes 4194320 | tf_op jit(solution)/shard_map/psum | solution.py:82
  750.1 6.0 multiply_subtract_fusion
  756.1 0.0 all-to-all-done.3
  756.1 13.0 %scatter_custom_fusion = f32[2048,256]{1,0:T(8,128)} fusion(s32[2048]{0:T(1024)S(1)} %reshape.90, f32[256,1,1,8,256]{4,3,2,1,0:T(8,128)S(1)} %all-to-all-done.3, f32[]{:T(128)} %constant.15.clone.1), kind=kCustom, calls=%fused_computation.7 | custom fusion | flops 524288 | bytes 4194308 | tf_op jit(solution)/shard_map/scatter-add | solution.py:76
  769.2 0.0 copy-start
  769.2 3.9 scatter_custom_fusion.2
  773.0 0.0 copy-done
  773.0 3.2 multiply_subtract_fusion.1
  (6 shorter events, 0.0 us)
Async XLA Ops:
  7.2 425.0 %all-gather.3.cloned.1.call-start = ((), (), s32[]{:S(2)}) async-start(), calls=%async_computation.5 | async-start | bytes 4210688 | tf_op jit(solution)/shard_map/all_gather | solution.py:39
  7.9 0.5 copy-start.6
  12.7 27.0 %all-to-all-start = ((s32[256,1,1,8]{3,2,1,0:T(1,128)}), s32[256,1,1,8]{3,2,1,0:T(1,128)S(1)}, u32[]{:S(2)}, u32[]{:S(2)}) async-start(s32[256,1,1,8]{3,2,1,0:T(1,128)} %bitcast), calls=%async_computation | async-start | bytes 262144 | tf_op jit(solution)/shard_map/all_to_all | solution.py:25
  81.6 5.7 copy-start.1
  81.6 6.6 copy-start.2
  81.6 6.8 copy-start.4
  82.6 18.3 %all-to-all-start.2 = ((bf16[64,4,8,256]{3,2,0,1:T(8,128)(2,1)}), bf16[64,4,8,256]{3,2,0,1:T(8,128)(2,1)S(1)}, u32[]{:S(2)}, u32[]{:S(2)}) async-start(bf16[64,4,8,256]{3,2,0,1:T(8,128)(2,1)} %copy.39), calls=%async_computation.2 | async-start | bytes 2097152 | tf_op jit(solution)/shard_map/all_to_all | solution.py:44
  442.0 2.8 copy-start.5
  448.2 9.6 %copy-start.3 = (s32[256,8]{0,1:T(8,128)S(1)}, s32[256,8]{0,1:T(8,128)}, u32[]{:S(2)}) copy-start(s32[256,8]{0,1:T(8,128)} %param.11) | copy-start | bytes 24580
  448.2 308.0 %all-to-all-start.3 = ((f32[256,1,1,8,256]{4,3,2,1,0:T(8,128)}), f32[256,1,1,8,256]{4,3,2,1,0:T(8,128)S(1)}, u32[]{:S(2)}, u32[]{:S(2)}) async-start(f32[256,1,1,8,256]{4,3,2,1,0:T(8,128)} %fusion.7), calls=%async_computation.3 | async-start | bytes 4194304 | tf_op jit(solution)/shard_map/all_to_all | solution.py:25
  457.5 292.6 %all-reduce.2.cloned.1.call-start = ((), (), s32[]{:S(2)}) async-start(), calls=%async_computation.4 | async-start | bytes 8388608 | tf_op jit(solution)/shard_map/psum | solution.py:82
  769.2 3.9 copy-start
Sparse Core Ops, SparseCore 0:
  11.3 420.7 all-gather.2
  472.0 278.0 all-reduce.1
where the time goes:
time: 784 us; the launch traced here: 783 us
  waiting for transfers between devices  630 us (80%)
  other arithmetic  45.5 us (6%)
  blocking collectives  34.3 us (4%)
  starting transfers between devices  29 us (4%)
  local copies, waits for them, and re-layouts  24.8 us (3%)
  between operations  14.2 us (2%)
    all_gather x1, waiting for transfers between devices, body(): lax.all_gather(table[hot_slot], ('rows', 'grp'), axis=0, tiled=True)  330 us
    psum x1, waiting for transfers between devices, body(): summed = lax.psum(hot_local, ('rows', 'grp'))  277 us
    all_to_all x1, blocking collectives, body(): lax.all_to_all(looked, 'rows', split_axis=0, concat_axis=0, tiled=True)  34.3 us
    all_to_all x2, starting transfers between devices, exchange_both(): lax.all_to_all(blocks, axis, split_axis=0, concat_axis=0, tiled=True)  24 us
  transfers between devices with their start and end apart: 5, of which 4 were waited for; matrix products, arithmetic and copies ran while one was open for 5% of the time, Pallas kernels for 0%

commit v1 on v0

--- a/solution.py
+++ b/solution.py
@@ -79,7 +79,7 @@
     hot_total = hot_copy.shape[0]
     spread = jnp.repeat(grad, hot_pick.shape[1], axis=0)
     hot_local = jax.ops.segment_sum(spread, hot_pick.reshape(-1), num_segments=hot_total)
-    summed = lax.psum(hot_local, ("rows", "grp"))
+    summed = lax.psum(lax.psum(hot_local, "rows"), "grp")
     start = lax.axis_index(("rows", "grp")) * own_hot
     own_grad = lax.dynamic_slice_in_dim(summed, start, own_hot, 0)
     table_grad = table_grad.at[hot_slot].add(own_grad)

time: 784 us -> 1300 us (1.66)
  waiting for transfers between devices: 630 us -> 1150 us
    psum x1 -> x2, waiting for transfers between devices: 277 us -> 746 us  [body(): summed = lax.psum(lax.psum(hot_local, 'rows'), 'grp')]
    all_to_all x2, waiting for transfers between devices: 10.6 us -> 61.2 us  [exchange_both(): lax.all_to_all(blocks, axis, split_axis=0, concat_axis=0, tiled=True)]
  transfers between devices with their start and end apart: 5 -> 6, of which waited for: 4 -> 6; matrix products, arithmetic and copies ran while one was open for 5% -> 2% of each run, Pallas kernels for 0% -> 0%
where the time goes in v1:
time: 1300 us
  waiting for transfers between devices  1150 us (88%)
  other arithmetic  44.4 us (3%)
  blocking collectives  34.3 us (3%)
  starting transfers between devices  29.3 us (2%)
  local copies, waits for them, and re-layouts  25.4 us (2%)
  between operations  13.9 us (1%)
    psum x2, waiting for transfers between devices, body(): summed = lax.psum(lax.psum(hot_local, 'rows'), 'grp')  746 us
    all_gather x1, waiting for transfers between devices, body(): lax.all_gather(table[hot_slot], ('rows', 'grp'), axis=0, tiled=True)  330 us
    all_to_all x2, waiting for transfers between devices, exchange_both(): lax.all_to_all(blocks, axis, split_axis=0, concat_axis=0, tiled=True)  61.2 us
    all_to_all x1, blocking collectives, body(): lax.all_to_all(looked, 'rows', split_axis=0, concat_axis=0, tiled=True)  34.3 us
  transfers between devices with their start and end apart: 6, of which 6 were waited for; matrix products, arithmetic and copies ran while one was open for 2% of the time, Pallas kernels for 0%

profile of v1, /device:TPU:2, one launch (start us, length us, event | category | flops | bytes accessed | tf_op | source)
XLA Modules:
  0.0 1301.0 jit_solution(3285122793624901062)
XLA Ops:
  7.2 0.0 all-gather.3.cloned.1.call-start
  7.2 0.7 compare_select_fusion.2
  7.9 0.0 copy-start.6
  7.9 0.6 copy-done.6
  8.5 2.8 gather_fusion.1
  11.2 0.0 all-gather.3.cloned.1.call-update
  11.2 1.5 copy.38
  12.7 14.7 %all-to-all-start = ((s32[256,1,1,8]{3,2,1,0:T(1,128)}), s32[256,1,1,8]{3,2,1,0:T(1,128)S(1)}, u32[]{:S(2)}, u32[]{:S(2)}) async-start(s32[256,1,1,8]{3,2,1,0:T(1,128)} %bitcast), calls=%async_computation | async-start | bytes 262144 | tf_op jit(solution)/shard_map/all_to_all | solution.py:25
  27.4 1.7 convert_element_type.14
  29.1 10.6 all-to-all-done
  39.7 0.2 reshape_reshape.6
  39.9 7.5 gather_fusion
  47.4 34.3 %all_to_all.20 = bf16[64,4,8,256]{3,2,1,0:T(8,128)(2,1)S(1)} all-to-all(bf16[64,4,8,256]{3,2,1,0:T(8,128)(2,1)S(1)} %bitcast.38), channel_id=1, replica_groups=mesh['rows'=64,'grp'=4] {'rows'}, dimensions={0} | all-to-all | bytes 2097152 | tf_op jit(solution)/shard_map/all_to_all | solution.py:45
  81.7 0.0 copy-start.2
  81.7 0.0 copy-start.3
  81.7 0.0 copy-start.4
  81.7 1.0 copy.39
  82.7 4.7 all-to-all-start.2
  87.4 0.0 all-reduce.3.cloned.1.call-start
  87.4 0.0 copy-done.2
  87.4 0.8 copy.43
  88.3 0.0 copy-done.3
  88.3 0.1 copy.45
  88.4 0.1 copy.41
  88.5 0.1 reshape.82
  88.6 0.0 copy-done.4
  88.6 0.1 copy.37
  88.8 0.1 eq.16
  88.9 0.7 reshape.98
  89.6 11.4 all-to-all-done.2
  101.0 1.1 copy.40
  102.1 330.1 %all-gather.3.cloned.1.call-done = f32[4096,256]{1,0:T(8,128)} async-done(((f32[16,256]{1,0:T(8,128)}), f32[4096,256]{1,0:T(8,128)}) %all-gather.3.cloned.1.call-update) | async-done | bytes 4194320 | tf_op jit(solution)/shard_map/all_gather | solution.py:39
  432.2 2.4 convert_element_type.15
  434.6 7.5 gather_fusion.2
  442.1 0.0 copy-start.5
  442.1 0.7 convert_reduce_fusion
  442.8 0.1 copy.42
  443.0 2.0 multiply_reduce_fusion
  445.0 0.0 copy-done.5
  445.0 0.1 broadcast_multiply_fusion
  445.1 14.0 %scatter_custom_fusion.1 = f32[4096,256]{1,0:T(8,128)} fusion(s32[2048]{0:T(1024)} %reshape.98, f32[]{:T(128)} %constant.15.clone.1, f32[256,256]{1,0:T(8,128)S(1)} %broadcast_multiply_fusion), kind=kCustom, calls=%fused_computation.10 | custom fusion | flops 524288 | bytes 4456960 | tf_op jit(solution)/shard_map/scatter-add | solution.py:81
  459.1 0.0 all-reduce.3.cloned.1.call-update
  459.1 0.0 all-reduce.5.cloned.1.call-start
  459.1 705.5 %all-reduce.3.cloned.1.call-done = f32[4096,256]{1,0:T(8,128)} async-done(((f32[4096,256]{1,0:T(8,128)}), f32[4096,256]{1,0:T(8,128)}) %all-reduce.3.cloned.1.call-update) | async-done | bytes 4194320 | tf_op jit(solution)/shard_map/psum | solution.py:82
  1164.7 0.0 all-reduce.5.cloned.1.call-update
  1164.7 3.2 fusion.7
  1167.9 9.8 all-to-all-start.3
  1177.7 0.2 reshape.90
  1177.8 0.8 copy.46
  1178.7 50.6 %all-to-all-done.3 = f32[256,1,1,8,256]{4,3,2,1,0:T(8,128)S(1)} async-done(((f32[256,1,1,8,256]{4,3,2,1,0:T(8,128)}), f32[256,1,1,8,256]{4,3,2,1,0:T(8,128)S(1)}, u32[]{:S(2)}, u32[]{:S(2)}) %all-to-all-start.3) | async-done | bytes 2097184 | tf_op jit(solution)/shard_map/all_to_all | solution.py:25
  1229.3 13.0 %scatter_custom_fusion = f32[2048,256]{1,0:T(8,128)} fusion(s32[2048]{0:T(1024)S(1)} %reshape.90, f32[256,1,1,8,256]{4,3,2,1,0:T(8,128)S(1)} %all-to-all-done.3, f32[]{:T(128)} %constant.15.clone.1), kind=kCustom, calls=%fused_computation.7 | custom fusion | flops 524288 | bytes 4194308 | tf_op jit(solution)/shard_map/scatter-add | solution.py:76
  1242.3 0.0 copy-start.1
  1242.3 40.4 %all-reduce.5.cloned.1.call-done = f32[4096,256]{1,0:T(8,128)} async-done(((f32[4096,256]{1,0:T(8,128)}), f32[4096,256]{1,0:T(8,128)}) %all-reduce.5.cloned.1.call-update) | async-done | bytes 4194320 | tf_op jit(solution)/shard_map/psum | solution.py:82
  1282.7 3.7 scatter_custom_fusion.2
  1286.4 0.0 copy-done.1
  1286.4 0.0 copy-start
  1286.4 3.3 multiply_subtract_fusion.1
  1289.7 0.0 copy-done
  1289.7 4.7 multiply_subtract_fusion
  (6 shorter events, 0.0 us)
Async XLA Ops:
  7.2 425.1 %all-gather.3.cloned.1.call-start = ((), (), s32[]{:S(2)}) async-start(), calls=%async_computation.6 | async-start | bytes 4210688 | tf_op jit(solution)/shard_map/all_gather | solution.py:39
  7.9 0.6 copy-start.6
  12.7 27.0 %all-to-all-start = ((s32[256,1,1,8]{3,2,1,0:T(1,128)}), s32[256,1,1,8]{3,2,1,0:T(1,128)S(1)}, u32[]{:S(2)}, u32[]{:S(2)}) async-start(s32[256,1,1,8]{3,2,1,0:T(1,128)} %bitcast), calls=%async_computation | async-start | bytes 262144 | tf_op jit(solution)/shard_map/all_to_all | solution.py:25
  81.7 5.8 copy-start.2
  81.7 6.6 copy-start.3
  81.7 7.0 copy-start.4
  82.7 18.3 %all-to-all-start.2 = ((bf16[64,4,8,256]{3,2,0,1:T(8,128)(2,1)}), bf16[64,4,8,256]{3,2,0,1:T(8,128)(2,1)S(1)}, u32[]{:S(2)}, u32[]{:S(2)}) async-start(bf16[64,4,8,256]{3,2,0,1:T(8,128)(2,1)} %copy.39), calls=%async_computation.2 | async-start | bytes 2097152 | tf_op jit(solution)/shard_map/all_to_all | solution.py:44
  87.4 1077.3 %all-reduce.3.cloned.1.call-start = ((), (), s32[]{:S(2)}) async-start(), calls=%async_computation.4 | async-start | bytes 8388608 | tf_op jit(solution)/shard_map/psum | solution.py:82
  442.1 2.8 copy-start.5
  459.1 823.6 %all-reduce.5.cloned.1.call-start = ((), (), s32[]{:S(2)}) async-start(), calls=%async_computation.5 | async-start | bytes 8388608 | tf_op jit(solution)/shard_map/psum | solution.py:82
  1167.9 61.4 %all-to-all-start.3 = ((f32[256,1,1,8,256]{4,3,2,1,0:T(8,128)}), f32[256,1,1,8,256]{4,3,2,1,0:T(8,128)S(1)}, u32[]{:S(2)}, u32[]{:S(2)}) async-start(f32[256,1,1,8,256]{4,3,2,1,0:T(8,128)} %fusion.7), calls=%async_computation.3 | async-start | bytes 4194304 | tf_op jit(solution)/shard_map/all_to_all | solution.py:25
  1242.3 44.1 %copy-start.1 = (f32[2048,256]{1,0:T(8,128)S(1)}, f32[2048,256]{1,0:T(8,128)}, u32[]{:S(2)}) copy-start(f32[2048,256]{1,0:T(8,128)} %param.7) | copy-start | bytes 6291460
  1286.4 3.3 copy-start
Sparse Core Ops, SparseCore 0:
  11.4 420.8 all-gather.2
  459.2 705.4 all-reduce.2
  1167.4 115.2 all-reduce.4
